TPU v7x, 32 devices: a whole 2x2x4 slice. The times are simulated.
32 devices in a mesh: lat: 8 (over y, x, core), lon: 4 (over z).
Axes of the slice: x: 2, y: 2, z: 4, core: 2. Of those that a mesh axis runs over, the one named last changes fastest.
Arguments:
- snapshots: float32 [1024, 128, 512], P(None, 'lat', 'lon'), may hold values from -60 to 60
- land_sea: int32 [128, 512], P('lat', 'lon'), may hold values 0 or 1
- penalty: float32 [128, 512], P('lat', 'lon'), may hold values from 0.003 to 0.03
- initial_basis: float32 [64, 128, 512], P(None, 'lat', 'lon'), may hold values from -6 to 6
Outputs:
- leading_basis: float32 [64, 128, 512], P(None, 'lat', 'lon')
- rayleigh_matrix: float32 [64, 64], replicated
All inputs are finite; a program needn't handle non-finite values. No bound on the sum of `land_sea` on one device may be relied on, other than what follows from the above.
Results may differ from a plain program's by a relative error of at most 0.0003.
Values sent between devices are 32-bit elements; how exact they have to be, the bound alone decides.
A program may use at most 64 MiB of HBM per device.

v0:
```python
import jax
import jax.numpy as jnp
from jax import lax
from jax.sharding import PartitionSpec as P

STEPS = 2


def padded_2(block, sides, width):
    for axis, dim in sides:
        count = lax.axis_size(axis)
        forward = [(i, i + 1) for i in range(count - 1)]
        backward = [(target, source) for source, target in forward]
        low = lax.ppermute(
            lax.slice_in_dim(block, block.shape[dim] - width, None, axis=dim), axis, forward
        )
        high = lax.ppermute(lax.slice_in_dim(block, 0, width, axis=dim), axis, backward)
        block = jnp.concatenate([low, block, high], axis=dim)
    return block


def laplacian(masked_field):
    padded = padded_2(masked_field, (("lat", 1), ("lon", 2)), 1)
    neighbours = (
        padded[:, 2:, 1:-1] + padded[:, :-2, 1:-1] + padded[:, 1:-1, 2:] + padded[:, 1:-1, :-2]
    )
    return neighbours - 4.0 * masked_field


def project_points(snapshots, masked_field):
    return jnp.einsum("tab,kab->tk", snapshots, masked_field, precision=lax.Precision.HIGHEST)


def expand_points(snapshots, coeffs):
    return jnp.einsum("tab,tk->kab", snapshots, coeffs, precision=lax.Precision.HIGHEST)


def inner_products(left_field, right_field):
    return jnp.einsum("kab,jab->kj", left_field, right_field, precision=lax.Precision.HIGHEST)


def apply_inverse(factor, stacked):
    solved = jax.scipy.linalg.solve_triangular(
        factor, stacked.reshape(stacked.shape[0], -1), lower=True
    )
    return solved.reshape(stacked.shape)


def total_terms(term_tuple):
    shares = (lax.psum_scatter(term_tuple[0], "lat", scatter_dimension=0, tiled=True),)
    summed = lax.psum((shares[0],), "lon")
    return (lax.all_gather(summed[0], "lat", axis=0, tiled=True),)


def local(snapshots, land_sea, penalty, initial_basis):
    ocean_mask = land_sea.astype(jnp.float32)
    point_count = float(
        snapshots.shape[1] * snapshots.shape[2] * lax.axis_size("lat") * lax.axis_size("lon")
    )
    current_basis = initial_basis * ocean_mask
    for iteration in range(STEPS):
        (coeffs,) = total_terms((project_points(snapshots, current_basis),))
        applied = ocean_mask * (
            expand_points(snapshots, coeffs) / point_count + penalty * laplacian(current_basis)
        )
        (moments,) = total_terms((inner_products(applied, applied),))
        factor = jnp.linalg.cholesky(moments / point_count)
        current_basis = apply_inverse(factor, applied)
    (coeffs,) = total_terms((project_points(snapshots, current_basis),))
    smoothed = laplacian(current_basis)
    final_image = ocean_mask * (expand_points(snapshots, coeffs) / point_count + penalty * smoothed)
    (projected,) = total_terms((inner_products(current_basis, final_image),))
    return (current_basis, projected / point_count)


def solution(mesh):
    in_specs = (P(None, "lat", "lon"), P("lat", "lon"), P("lat", "lon"), P(None, "lat", "lon"))
    out_specs = (P(None, "lat", "lon"), P())
    return jax.shard_map(local, mesh=mesh, in_specs=in_specs, out_specs=out_specs, check_vma=False)
```

profile of v0, /device:TPU:0, one launch (start us, length us, event | category | flops | bytes accessed | tf_op | source)
XLA Modules:
  0.0 464.0 jit_solution(17767832957010539441)
XLA Ops:
  10.5 3.0 collective-permute-start.1
  13.5 12.8 %fusion.39 = f32[1024,64]{0,1:T(8,128)} fusion(f32[64,16,128]{2,0,1:T(8,128)S(1)} %copy_multiply_fusion, f32[1024,16,128]{2,1,0:T(8,128)} %param.7), kind=kOutput, calls=%fused_computation.22 | convolution fusion | flops 1610612736 | bytes 9175040 | tf_op jit(solution)/shard_map/tab,kab->tk/dot_general | solution.py:31
  28.5 5.6 %collective-permute-start.3 = (f32[64,18,1]{0,2,1:T(1,128)S(1)}, f32[64,18,1]{0,2,1:T(1,128)S(1)}, u32[]{:S(2)}, u32[]{:S(2)}) collective-permute-start(f32[64,18,1]{0,2,1:T(1,128)S(1)} %copy.45), channel_id=1, source_target_pairs={{0,1},{1,2},{2,3},{4,5},{5,6},{6,7},{8,9},{9,10},{10,11},{12,13},{... | collective-permute-start | bytes 13832 | tf_op jit(solution)/shard_map/ppermute | solution.py:14
  35.9 27.7 %reduce-scatter.7.cloned.1.call-done = f32[128,64]{0,1:T(8,128)} async-done(((f32[1024,64]{0,1:T(8,128)}), f32[128,64]{0,1:T(8,128)}) %reduce-scatter.7.cloned.1.call-update) | async-done | bytes 32784 | tf_op jit(solution)/shard_map/reduce_scatter | solution.py:50
  63.6 19.6 %psum.42 = f32[128,64]{0,1:T(8,128)S(1)} all-reduce(f32[128,64]{0,1:T(8,128)} %reduce-scatter.7.cloned.1.call-done), channel_id=1, replica_groups=mesh['lat'=8,'lon'=4] {'lon'}, use_global_device_ids=true, to_apply=%region_1.0 | all-reduce | flops 8192 | bytes 65536 | tf_op jit(solution)/shard_map/psum | solution.py:51
  83.2 9.8 %all_gather.18 = f32[1024,64]{0,1:T(8,128)S(1)} all-gather(f32[128,64]{0,1:T(8,128)S(1)} %psum.42), channel_id=1, replica_groups=mesh['lat'=8,'lon'=4] {'lat'}, dimensions={0}, use_global_device_ids=true | all-gather | bytes 294912 | tf_op jit(solution)/shard_map/all_gather | solution.py:52
  93.0 9.8 %fusion.36 = f32[64,16,128]{2,0,1:T(8,128)S(1)} fusion(f32[1024,16,128]{2,1,0:T(8,128)} %param.7, f32[64,18,1]{2,0,1:T(8,128)S(1)} %copy.46, f32[64,1,128]{2,0,1:T(8,128)S(1)} %collective-permute-done, f32[64,16,128]{2,0,1:T(8,128)S(1)} %copy_multiply_fusion, f32[64,1,128]{2,0,1:T(8,128)S(1)} %collective-permute-done.1, f32[64,18,1]{2,0,1:T(8,128)S(1)} %copy.44, ...), kind=kOutput, calls=%fused_computation.20 | convolution fusion | flops 1612840960 | bytes 9790464 | tf_op jit(solution)/shard_map/tab,tk->kab/dot_general | solution.py:35
  103.4 23.6 %all-reduce = f32[64,64]{0,1:T(8,128)S(1)} all-reduce(f32[64,64]{0,1:T(8,128)S(1)} %convolution_bitcast_fusion.3), channel_id=3, replica_groups=mesh['lat'=8,'lon'=4] {'lat'}, use_global_device_ids=true, to_apply=%region_2.0.clone | all-reduce | flops 4096 | bytes 32768
  127.0 15.8 %psum.43 = f32[8,64]{0,1:T(8,128)S(1)} all-reduce(f32[8,64]{0,1:T(8,128)S(1)} %constant_dynamic-slice_fusion.2), channel_id=1, replica_groups=mesh['lat'=8,'lon'=4] {'lon'}, use_global_device_ids=true, to_apply=%region_3.0 | all-reduce | flops 512 | bytes 4096 | tf_op jit(solution)/shard_map/psum | solution.py:51
  142.9 8.6 %all_gather.19 = f32[64,64]{1,0:T(8,128)S(1)} all-gather(f32[8,64]{1,0:T(8,128)S(1)} %copy.48), channel_id=1, replica_groups=mesh['lat'=8,'lon'=4] {'lat'}, dimensions={0}, use_global_device_ids=true | all-gather | bytes 18432 | tf_op jit(solution)/shard_map/all_gather | solution.py:52
  151.7 5.8 %cholesky.44 = f32[64,64]{1,0:T(8,128)S(1)} custom-call(f32[64,64]{1,0:T(8,128)S(1)} %fusion.76), custom_call_target="Cholesky" | custom-call | tf_op jit(solution)/shard_map/jit(cholesky)/cholesky | solution.py:67
  158.8 4.9 %custom-call.6 = f32[1,64,64]{1,2,0:T(8,128)S(1)} custom-call(f32[1,64,64]{2,1,0:T(8,128)S(1)} %fusion.71), custom_call_target="InvertDiagBlocksLowerTriangular" | custom-call | tf_op jit(solution)/shard_map/jit(_solve_triangular)/triangular_solve | solution.py:43
  166.7 12.8 %fusion.42 = f32[1024,64]{0,1:T(8,128)} fusion(f32[1024,16,128]{2,1,0:T(8,128)} %param.7, f32[8,16,8,128]{3,2,1,0:T(8,128)S(1)} %convolution_bitcast_fusion), kind=kOutput, calls=%fused_computation.23 | convolution fusion | flops 1610612736 | bytes 9175040 | tf_op jit(solution)/shard_map/tab,kab->tk/dot_general | solution.py:31
  185.4 4.6 collective-permute-start.7
  191.5 24.7 %reduce-scatter.9.cloned.1.call-done = f32[128,64]{0,1:T(8,128)} async-done(((f32[1024,64]{0,1:T(8,128)}), f32[128,64]{0,1:T(8,128)}) %reduce-scatter.9.cloned.1.call-update) | async-done | bytes 32784 | tf_op jit(solution)/shard_map/reduce_scatter | solution.py:50
  216.3 19.6 %psum.44 = f32[128,64]{0,1:T(8,128)S(1)} all-reduce(f32[128,64]{0,1:T(8,128)} %reduce-scatter.9.cloned.1.call-done), channel_id=1, replica_groups=mesh['lat'=8,'lon'=4] {'lon'}, use_global_device_ids=true, to_apply=%region_7.0 | all-reduce | flops 8192 | bytes 65536 | tf_op jit(solution)/shard_map/psum | solution.py:51
  235.9 10.0 %all_gather.20 = f32[1024,64]{0,1:T(8,128)S(1)} all-gather(f32[128,64]{0,1:T(8,128)S(1)} %psum.44), channel_id=1, replica_groups=mesh['lat'=8,'lon'=4] {'lat'}, dimensions={0}, use_global_device_ids=true | all-gather | bytes 294912 | tf_op jit(solution)/shard_map/all_gather | solution.py:52
  245.9 9.8 %fusion.33 = f32[64,16,128]{2,0,1:T(8,128)S(1)} fusion(f32[1024,16,128]{2,1,0:T(8,128)} %param.7, f32[64,18,128]{2,0,1:T(8,128)S(1)} %constant_dynamic-update-slice_fusion, f32[64,18,1]{2,0,1:T(8,128)S(1)} %copy.63, f32[64,18,1]{2,0,1:T(8,128)S(1)} %copy.61, f32[64,16,128]{2,0,1:T(8,128)S(1)} %bitcast.101, f32[64,1,128]{2,0,1:T(8,128)S(1)} %collective-permute-done.5, ...), kind=kOutput, calls=%fused_computation.19 | convolution fusion | flops 1612316672 | bytes 10380288 | tf_op jit(solution)/shard_map/tab,tk->kab/dot_general | solution.py:35
  256.3 23.6 %all-reduce.1 = f32[64,64]{0,1:T(8,128)S(1)} all-reduce(f32[64,64]{0,1:T(8,128)S(1)} %convolution_bitcast_fusion.2), channel_id=5, replica_groups=mesh['lat'=8,'lon'=4] {'lat'}, use_global_device_ids=true, to_apply=%region_8.0.clone | all-reduce | flops 4096 | bytes 32768
  280.0 15.8 %psum.45 = f32[8,64]{0,1:T(8,128)S(1)} all-reduce(f32[8,64]{0,1:T(8,128)S(1)} %constant_dynamic-slice_fusion.1), channel_id=1, replica_groups=mesh['lat'=8,'lon'=4] {'lon'}, use_global_device_ids=true, to_apply=%region_9.0 | all-reduce | flops 512 | bytes 4096 | tf_op jit(solution)/shard_map/psum | solution.py:51
  295.8 8.1 %all_gather.21 = f32[64,64]{1,0:T(8,128)S(1)} all-gather(f32[8,64]{1,0:T(8,128)S(1)} %copy.66), channel_id=1, replica_groups=mesh['lat'=8,'lon'=4] {'lat'}, dimensions={0}, use_global_device_ids=true | all-gather | bytes 18432 | tf_op jit(solution)/shard_map/all_gather | solution.py:52
  304.1 5.8 %cholesky.55 = f32[64,64]{1,0:T(8,128)S(1)} custom-call(f32[64,64]{1,0:T(8,128)S(1)} %fusion.74), custom_call_target="Cholesky" | custom-call | tf_op jit(solution)/shard_map/jit(cholesky)/cholesky | solution.py:67
  311.3 4.9 %custom-call.7 = f32[1,64,64]{1,2,0:T(8,128)S(1)} custom-call(f32[1,64,64]{2,1,0:T(8,128)S(1)} %fusion.72), custom_call_target="InvertDiagBlocksLowerTriangular" | custom-call | tf_op jit(solution)/shard_map/jit(_solve_triangular)/triangular_solve | solution.py:43
  319.2 12.8 %fusion.45 = f32[1024,64]{0,1:T(8,128)} fusion(f32[1024,16,128]{2,1,0:T(8,128)} %param.7, f32[64,2048]{1,0:T(8,128)S(1)} %fusion.48), kind=kOutput, calls=%fused_computation.24 | convolution fusion | flops 1610612736 | bytes 9175040 | tf_op jit(solution)/shard_map/tab,kab->tk/dot_general | solution.py:31
  337.8 4.6 collective-permute-start.11
  344.0 24.9 %reduce-scatter.11.cloned.1.call-done = f32[128,64]{0,1:T(8,128)} async-done(((f32[1024,64]{0,1:T(8,128)}), f32[128,64]{0,1:T(8,128)}) %reduce-scatter.11.cloned.1.call-update) | async-done | bytes 32784 | tf_op jit(solution)/shard_map/reduce_scatter | solution.py:50
  368.9 19.6 %psum.46 = f32[128,64]{0,1:T(8,128)S(1)} all-reduce(f32[128,64]{0,1:T(8,128)} %reduce-scatter.11.cloned.1.call-done), channel_id=1, replica_groups=mesh['lat'=8,'lon'=4] {'lon'}, use_global_device_ids=true, to_apply=%region_11.0 | all-reduce | flops 8192 | bytes 65536 | tf_op jit(solution)/shard_map/psum | solution.py:51
  388.5 9.8 %all_gather.22 = f32[1024,64]{0,1:T(8,128)S(1)} all-gather(f32[128,64]{0,1:T(8,128)S(1)} %psum.46), channel_id=1, replica_groups=mesh['lat'=8,'lon'=4] {'lat'}, dimensions={0}, use_global_device_ids=true | all-gather | bytes 294912 | tf_op jit(solution)/shard_map/all_gather | solution.py:52
  398.4 9.8 %fusion.30 = f32[64,16,128]{2,0,1:T(8,128)S(1)} fusion(f32[1024,16,128]{2,1,0:T(8,128)} %param.7, f32[64,18,128]{2,0,1:T(8,128)S(1)} %constant_dynamic-update-slice_fusion.3, f32[64,18,1]{2,0,1:T(8,128)S(1)} %copy.81, f32[64,18,1]{2,0,1:T(8,128)S(1)} %copy.79, f32[64,16,128]{2,0,1:T(8,128)S(1)} %copy_bitcast_fusion, ...), kind=kOutput, calls=%fused_computation.18 | convolution fusion | flops 1612316672 | bytes 10380288 | tf_op jit(solution)/shard_map/tab,tk->kab/dot_general | solution.py:35
  408.8 23.6 %all-reduce.2 = f32[64,64]{0,1:T(8,128)S(1)} all-reduce(f32[64,64]{0,1:T(8,128)S(1)} %convolution_bitcast_fusion.1), channel_id=7, replica_groups=mesh['lat'=8,'lon'=4] {'lat'}, use_global_device_ids=true, to_apply=%region_12.15.clone | all-reduce | flops 4096 | bytes 32768
  432.5 15.8 %psum.47 = f32[8,64]{0,1:T(8,128)S(1)} all-reduce(f32[8,64]{0,1:T(8,128)S(1)} %constant_dynamic-slice_fusion), channel_id=1, replica_groups=mesh['lat'=8,'lon'=4] {'lon'}, use_global_device_ids=true, to_apply=%region_13.16 | all-reduce | flops 512 | bytes 4096 | tf_op jit(solution)/shard_map/psum | solution.py:51
  448.3 8.1 %all_gather.23 = f32[64,64]{1,0:T(8,128)S(1)} all-gather(f32[8,64]{1,0:T(8,128)S(1)} %copy.85), channel_id=1, replica_groups=mesh['lat'=8,'lon'=4] {'lat'}, dimensions={0}, use_global_device_ids=true | all-gather | bytes 18432 | tf_op jit(solution)/shard_map/all_gather | solution.py:52
  (89 shorter events, 32.9 us)
Async XLA Ops:
  7.2 26.9 %copy-start.1 = (u32[32]{0:T(128)S(1)}, u32[32]{0:T(128)}, u32[]{:S(2)}) copy-start(u32[32]{0:T(128)} %constant.44) | copy-start | bytes 388
  7.2 56.4 %reduce-scatter.7.cloned.1.call-start = ((), (), s32[]{:S(2)}) async-start(), calls=%async_computation.3 | async-start | bytes 294912 | tf_op jit(solution)/shard_map/reduce_scatter | solution.py:50
  7.9 85.1 %copy-start = (f32[16,128]{1,0:T(8,128)S(1)}, f32[16,128]{1,0:T(8,128)}, u32[]{:S(2)}) copy-start(f32[16,128]{1,0:T(8,128)} %param.9) | copy-start | bytes 24580
  9.2 17.2 %collective-permute-start = (f32[64,1,128]{2,0,1:T(8,128)S(1)}, f32[64,1,128]{2,0,1:T(8,128)S(1)}, u32[]{:S(2)}, u32[]{:S(2)}) collective-permute-start(f32[64,1,128]{2,0,1:T(8,128)S(1)} %get-tuple-element.21), channel_id=1, source_target_pairs={{4,0},{8,4},{12,8},{16,12},{20,16},{24,20},{28,24},{5,1},{9,5},{13... | collective-permute-start | bytes 98312 | tf_op jit(solution)/shard_map/ppermute | solution.py:17
  10.5 16.0 %collective-permute-start.1 = (f32[64,1,128]{2,0,1:T(8,128)S(1)}, f32[64,1,128]{2,0,1:T(8,128)S(1)}, u32[]{:S(2)}, u32[]{:S(2)}) collective-permute-start(f32[64,1,128]{2,0,1:T(8,128)S(1)} %get-tuple-element.20), channel_id=1, source_target_pairs={{0,4},{4,8},{8,12},{12,16},{16,20},{20,24},{24,28},{1,5},{5,9},{9,... | collective-permute-start | bytes 98312 | tf_op jit(solution)/shard_map/ppermute | solution.py:14
  26.4 189.9 %reduce-scatter.9.cloned.1.call-start = ((), (), s32[]{:S(2)}) async-start(), calls=%async_computation.4 | async-start | bytes 294912 | tf_op jit(solution)/shard_map/reduce_scatter | solution.py:50
  26.9 8.4 %collective-permute-start.2 = (f32[64,18,1]{0,2,1:T(1,128)S(1)}, f32[64,18,1]{0,2,1:T(1,128)S(1)}, u32[]{:S(2)}, u32[]{:S(2)}) collective-permute-start(f32[64,18,1]{0,2,1:T(1,128)S(1)} %copy.43), channel_id=1, source_target_pairs={{1,0},{2,1},{3,2},{5,4},{6,5},{7,6},{9,8},{10,9},{11,10},{13,12},{... | collective-permute-start | bytes 13832 | tf_op jit(solution)/shard_map/ppermute | solution.py:17
  28.5 7.1 %collective-permute-start.3 = (f32[64,18,1]{0,2,1:T(1,128)S(1)}, f32[64,18,1]{0,2,1:T(1,128)S(1)}, u32[]{:S(2)}, u32[]{:S(2)}) collective-permute-start(f32[64,18,1]{0,2,1:T(1,128)S(1)} %copy.45), channel_id=1, source_target_pairs={{0,1},{1,2},{2,3},{4,5},{5,6},{6,7},{8,9},{9,10},{10,11},{12,13},{... | collective-permute-start | bytes 13832 | tf_op jit(solution)/shard_map/ppermute | solution.py:14
  164.5 16.5 %collective-permute-start.5 = (f32[64,1,128]{2,0,1:T(8,128)S(1)}, f32[64,1,128]{2,0,1:T(8,128)S(1)}, u32[]{:S(2)}, u32[]{:S(2)}) collective-permute-start(f32[64,1,128]{2,0,1:T(8,128)S(1)} %get-tuple-element.19), channel_id=1, source_target_pairs={{0,4},{4,8},{8,12},{12,16},{16,20},{20,24},{24,28},{1,5},{5,9},{9,... | collective-permute-start | bytes 98312 | tf_op jit(solution)/shard_map/ppermute | solution.py:14
  179.6 3.8 collective-permute-start.4
  180.9 188.1 %reduce-scatter.11.cloned.1.call-start = ((), (), s32[]{:S(2)}) async-start(), calls=%async_computation.5 | async-start | bytes 294912 | tf_op jit(solution)/shard_map/reduce_scatter | solution.py:50
  183.8 6.1 %collective-permute-start.6 = (f32[64,18,1]{0,2,1:T(1,128)S(1)}, f32[64,18,1]{0,2,1:T(1,128)S(1)}, u32[]{:S(2)}, u32[]{:S(2)}) collective-permute-start(f32[64,18,1]{0,2,1:T(1,128)S(1)} %copy.60), channel_id=1, source_target_pairs={{1,0},{2,1},{3,2},{5,4},{6,5},{7,6},{9,8},{10,9},{11,10},{13,12},{... | collective-permute-start | bytes 13832 | tf_op jit(solution)/shard_map/ppermute | solution.py:17
  185.4 5.9 %collective-permute-start.7 = (f32[64,18,1]{0,2,1:T(1,128)S(1)}, f32[64,18,1]{0,2,1:T(1,128)S(1)}, u32[]{:S(2)}, u32[]{:S(2)}) collective-permute-start(f32[64,18,1]{0,2,1:T(1,128)S(1)} %copy.62), channel_id=1, source_target_pairs={{0,1},{1,2},{2,3},{4,5},{5,6},{6,7},{8,9},{9,10},{10,11},{12,13},{... | collective-permute-start | bytes 13832 | tf_op jit(solution)/shard_map/ppermute | solution.py:14
  316.9 16.6 %collective-permute-start.9 = (f32[64,1,128]{2,0,1:T(8,128)S(1)}, f32[64,1,128]{2,0,1:T(8,128)S(1)}, u32[]{:S(2)}, u32[]{:S(2)}) collective-permute-start(f32[64,1,128]{2,0,1:T(8,128)S(1)} %get-tuple-element.17), channel_id=1, source_target_pairs={{0,4},{4,8},{8,12},{12,16},{16,20},{20,24},{24,28},{1,5},{5,9},{9,... | collective-permute-start | bytes 98312 | tf_op jit(solution)/shard_map/ppermute | solution.py:14
  332.0 3.8 collective-permute-start.8
  336.3 7.0 %collective-permute-start.10 = (f32[64,18,1]{0,2,1:T(1,128)S(1)}, f32[64,18,1]{0,2,1:T(1,128)S(1)}, u32[]{:S(2)}, u32[]{:S(2)}) collective-permute-start(f32[64,18,1]{0,2,1:T(1,128)S(1)} %copy.78), channel_id=1, source_target_pairs={{1,0},{2,1},{3,2},{5,4},{6,5},{7,6},{9,8},{10,9},{11,10},{13,12},{... | collective-permute-start | bytes 13832 | tf_op jit(solution)/shard_map/ppermute | solution.py:17
  337.8 5.9 %collective-permute-start.11 = (f32[64,18,1]{0,2,1:T(1,128)S(1)}, f32[64,18,1]{0,2,1:T(1,128)S(1)}, u32[]{:S(2)}, u32[]{:S(2)}) collective-permute-start(f32[64,18,1]{0,2,1:T(1,128)S(1)} %copy.80), channel_id=1, source_target_pairs={{0,1},{1,2},{2,3},{4,5},{5,6},{6,7},{8,9},{9,10},{10,11},{12,13},{... | collective-permute-start | bytes 13832 | tf_op jit(solution)/shard_map/ppermute | solution.py:14
Sparse Core Ops, SparseCore 0:
  26.5 37.0 reduce-scatter.6
  181.0 35.2 reduce-scatter.8
  333.6 35.2 reduce-scatter.10
where the time goes:
time: 473 us; the launch traced here: 464 us
  blocking collectives  231 us (49%)
  waiting for transfers between devices  83.4 us (18%)
  matrix products  70.9 us (15%)
  starting transfers between devices  30.3 us (6%)
  other arithmetic  26.2 us (6%)
  between operations  15.1 us (3%)
  local copies, waits for them, and re-layouts  6.75 us (1%)
    psum x6, blocking collectives, total_terms(): summed = lax.psum((shares[0],), 'lon')  106 us
    reduce_scatter x3, waiting for transfers between devices, total_terms(): lax.psum_scatter(term_tuple[0], 'lat', scatter_dimension=0, tiled=True)  77.4 us
    unnamed x3, blocking collectives  70.8 us
    all_gather x6, blocking collectives, total_terms(): return (lax.all_gather(summed[0], 'lat', axis=0, tiled=True),)  54.5 us
    dot_general x3, matrix products, project_points(): jnp.einsum('tab,kab->tk', snapshots, masked_field, precision=lax.Precisio...  38.5 us
    dot_general x3, matrix products, expand_points(): jnp.einsum('tab,tk->kab', snapshots, coeffs, precision=lax.Precision.HIGH...  29.4 us
    ppermute x6, starting transfers between devices, padded_2(): lax.ppermute(lax.slice_in_dim(block, block.shape[dim] - width, None, axis...  22.2 us
    another operation x6, other arithmetic, local(): factor = jnp.linalg.cholesky(moments / point_count)  13 us
  transfers between devices with their start and end apart: 15, of which 7 were waited for; matrix products, arithmetic and copies ran while one was open for 9% of the time, Pallas kernels for 0%

commit v1 on v0

--- a/solution.py
+++ b/solution.py
@@ -4,6 +4,27 @@
 from jax.sharding import PartitionSpec as P
 
 STEPS = 2
+
+
+def gather_around(x, axis, dim):
+    size, index, span = (lax.axis_size(axis), lax.axis_index(axis), x.shape[dim])
+    ahead = [(i, (i + 1) % size) for i in range(size)]
+    left = [(i, (i - 1) % size) for i in range(size)]
+    whole = jnp.zeros((*x.shape[:dim], size * span, *x.shape[dim + 1 :]), x.dtype)
+    whole = lax.dynamic_update_slice_in_dim(whole, x, index * span, axis=dim)
+    from_left = from_right = x
+    middle = size // 2
+    for hop in range(1, middle + 1):
+        from_left = lax.ppermute(from_left, axis, ahead)
+        whole = lax.dynamic_update_slice_in_dim(
+            whole, from_left, (index - hop) % size * span, axis=dim
+        )
+        if hop < size - middle:
+            from_right = lax.ppermute(from_right, axis, left)
+            whole = lax.dynamic_update_slice_in_dim(
+                whole, from_right, (index + hop) % size * span, axis=dim
+            )
+    return whole
 
 
 def padded_2(block, sides, width):
@@ -49,7 +70,7 @@
 def total_terms(term_tuple):
     shares = (lax.psum_scatter(term_tuple[0], "lat", scatter_dimension=0, tiled=True),)
     summed = lax.psum((shares[0],), "lon")
-    return (lax.all_gather(summed[0], "lat", axis=0, tiled=True),)
+    return (gather_around(summed[0], "lat", 0),)
 
 
 def local(snapshots, land_sea, penalty, initial_basis):

time: 473 us -> 512 us (1.082)
  blocking collectives: 231 us -> 173 us
  starting transfers between devices: 30.3 us -> 77 us
  waiting for transfers between devices: 83.4 us -> 123 us
  local copies, waits for them, and re-layouts: 6.75 us -> 16.6 us
    all_gather x6 -> x0, blocking collectives: 54.5 us -> none  [total_terms(): return (lax.all_gather(summed[0], 'lat', axis=0, tiled=True),)]
    ppermute x0 -> x42, starting transfers between devices: none -> 48.6 us  [the longest x18 47.6 us: gather_around(): from_right = lax.ppermute(from_right, axis, left)]
    ppermute x0 -> x42, waiting for transfers between devices: none -> 43.8 us  [the longest x24 43.7 us: gather_around(): from_left = lax.ppermute(from_left, axis, ahead)]
    dynamic_update_slice x0 -> x48, local copies, waits for them, and re-layouts: none -> 10.2 us  [the longest x24 5.27 us: gather_around(): lax.dynamic_update_slice_in_dim(whole, from_left, (index - hop) % size *...]
  transfers between devices with their start and end apart: 15 -> 57, of which waited for: 7 -> 31; matrix products, arithmetic and copies ran while one was open for 9% -> 10% of each run, Pallas kernels for 0% -> 0%
where the time goes in v1:
time: 512 us; the launch traced here: 503 us
  blocking collectives  173 us (34%)
  waiting for transfers between devices  123 us (24%)
  starting transfers between devices  77 us (15%)
  matrix products  70.9 us (14%)
  other arithmetic  26.1 us (5%)
  local copies, waits for them, and re-layouts  16.6 us (3%)
  between operations  15.8 us (3%)
    psum x6, blocking collectives, total_terms(): summed = lax.psum((shares[0],), 'lon')  106 us
    reduce_scatter x3, waiting for transfers between devices, total_terms(): lax.psum_scatter(term_tuple[0], 'lat', scatter_dimension=0, tiled=True)  73.7 us
    unnamed x3, blocking collectives  67.1 us
    ppermute x18, starting transfers between devices, gather_around(): from_right = lax.ppermute(from_right, axis, left)  47.6 us
    ppermute x24, waiting for transfers between devices, gather_around(): from_left = lax.ppermute(from_left, axis, ahead)  43.7 us
    dot_general x3, matrix products, project_points(): jnp.einsum('tab,kab->tk', snapshots, masked_field, precision=lax.Precisio...  38.5 us
    dot_general x3, matrix products, expand_points(): jnp.einsum('tab,tk->kab', snapshots, coeffs, precision=lax.Precision.HIGH...  29.5 us
    ppermute x6, starting transfers between devices, padded_2(): lax.ppermute(lax.slice_in_dim(block, block.shape[dim] - width, None, axis...  20.5 us
  transfers between devices with their start and end apart: 57, of which 31 were waited for; matrix products, arithmetic and copies ran while one was open for 10% of the time, Pallas kernels for 0%

profile of v1, /device:TPU:0, one launch (start us, length us, event | category | flops | bytes accessed | tf_op | source)
XLA Modules:
  0.0 502.9 jit_solution(12947546365785691878)
XLA Ops:
  10.5 3.0 collective-permute-start.8
  13.5 12.8 %fusion.39 = f32[1024,64]{0,1:T(8,128)} fusion(f32[64,16,128]{2,0,1:T(8,128)S(1)} %copy_multiply_fusion, f32[1024,16,128]{2,1,0:T(8,128)} %param.7), kind=kOutput, calls=%fused_computation.22 | convolution fusion | flops 1610612736 | bytes 9175040 | tf_op jit(solution)/shard_map/tab,kab->tk/dot_general | solution.py:52
  28.5 5.6 %collective-permute-start.10 = (f32[64,18,1]{0,2,1:T(1,128)S(1)}, f32[64,18,1]{0,2,1:T(1,128)S(1)}, u32[]{:S(2)}, u32[]{:S(2)}) collective-permute-start(f32[64,18,1]{0,2,1:T(1,128)S(1)} %copy.53), channel_id=1, source_target_pairs={{0,1},{1,2},{2,3},{4,5},{5,6},{6,7},{8,9},{9,10},{10,11},{12,13},{... | collective-permute-start | bytes 13832 | tf_op jit(solution)/shard_map/ppermute | solution.py:35
  36.0 27.6 %reduce-scatter.7.cloned.1.call-done = f32[128,64]{0,1:T(8,128)} async-done(((f32[1024,64]{0,1:T(8,128)}), f32[128,64]{0,1:T(8,128)}) %reduce-scatter.7.cloned.1.call-update) | async-done | bytes 32784 | tf_op jit(solution)/shard_map/reduce_scatter | solution.py:71
  63.6 19.6 %psum.42 = f32[128,64]{0,1:T(8,128)S(1)} all-reduce(f32[128,64]{0,1:T(8,128)} %reduce-scatter.7.cloned.1.call-done), channel_id=1, replica_groups=mesh['lat'=8,'lon'=4] {'lon'}, use_global_device_ids=true, to_apply=%region_1.0 | all-reduce | flops 8192 | bytes 65536 | tf_op jit(solution)/shard_map/psum | solution.py:72
  96.1 4.2 collective-permute-done.6
  100.4 9.8 %fusion.36 = f32[64,16,128]{2,0,1:T(8,128)S(1)} fusion(f32[1024,16,128]{2,1,0:T(8,128)} %param.7, f32[64,18,1]{2,0,1:T(8,128)S(1)} %copy.54, f32[64,1,128]{2,0,1:T(8,128)S(1)} %collective-permute-done.7, f32[64,16,128]{2,0,1:T(8,128)S(1)} %copy_multiply_fusion, f32[64,1,128]{2,0,1:T(8,128)S(1)} %collective-permute-done.8, f32[64,18,1]{2,0,1:T(8,128)S(1)} %copy.52, ...), kind=kOutput, calls=%fused_computation.20 | convolution fusion | flops 1612840960 | bytes 9790464 | tf_op jit(solution)/shard_map/tab,tk->kab/dot_general | solution.py:56
  110.7 22.4 %all-reduce = f32[64,64]{0,1:T(8,128)S(1)} all-reduce(f32[64,64]{0,1:T(8,128)S(1)} %convolution_bitcast_fusion.3), channel_id=3, replica_groups=mesh['lat'=8,'lon'=4] {'lat'}, use_global_device_ids=true, to_apply=%region_2.3.clone | all-reduce | flops 4096 | bytes 32768
  133.2 15.8 %psum.43 = f32[8,64]{0,1:T(8,128)S(1)} all-reduce(f32[8,64]{0,1:T(8,128)S(1)} %constant_dynamic-slice_fusion.2), channel_id=1, replica_groups=mesh['lat'=8,'lon'=4] {'lon'}, use_global_device_ids=true, to_apply=%region_3.4 | all-reduce | flops 512 | bytes 4096 | tf_op jit(solution)/shard_map/psum | solution.py:72
  166.9 5.8 %cholesky.44 = f32[64,64]{1,0:T(8,128)S(1)} custom-call(f32[64,64]{1,0:T(8,128)S(1)} %fusion.76), custom_call_target="Cholesky" | custom-call | tf_op jit(solution)/shard_map/jit(cholesky)/cholesky | solution.py:88
  174.1 4.9 custom-call.6
  181.0 12.8 %fusion.42 = f32[1024,64]{0,1:T(8,128)} fusion(f32[1024,16,128]{2,1,0:T(8,128)} %param.7, f32[8,16,8,128]{3,2,1,0:T(8,128)S(1)} %convolution_bitcast_fusion), kind=kOutput, calls=%fused_computation.23 | convolution fusion | flops 1610612736 | bytes 9175040 | tf_op jit(solution)/shard_map/tab,kab->tk/dot_general | solution.py:52
  199.0 4.6 collective-permute-start.28
  205.1 23.0 %reduce-scatter.9.cloned.1.call-done = f32[128,64]{0,1:T(8,128)} async-done(((f32[1024,64]{0,1:T(8,128)}), f32[128,64]{0,1:T(8,128)}) %reduce-scatter.9.cloned.1.call-update) | async-done | bytes 32784 | tf_op jit(solution)/shard_map/reduce_scatter | solution.py:71
  228.2 19.6 %psum.44 = f32[128,64]{0,1:T(8,128)S(1)} all-reduce(f32[128,64]{0,1:T(8,128)} %reduce-scatter.9.cloned.1.call-done), channel_id=1, replica_groups=mesh['lat'=8,'lon'=4] {'lon'}, use_global_device_ids=true, to_apply=%region_7.10 | all-reduce | flops 8192 | bytes 65536 | tf_op jit(solution)/shard_map/psum | solution.py:72
  252.1 2.7 collective-permute-start.21
  256.4 2.7 collective-permute-start.23
  260.9 4.2 collective-permute-done.24
  265.0 9.8 %fusion.33 = f32[64,16,128]{2,0,1:T(8,128)S(1)} fusion(f32[1024,16,128]{2,1,0:T(8,128)} %param.7, f32[64,18,128]{2,0,1:T(8,128)S(1)} %constant_dynamic-update-slice_fusion, f32[64,18,1]{2,0,1:T(8,128)S(1)} %copy.69, f32[64,18,1]{2,0,1:T(8,128)S(1)} %copy.67, f32[64,16,128]{2,0,1:T(8,128)S(1)} %bitcast.101, f32[64,1,128]{2,0,1:T(8,128)S(1)} %collective-permute-done.26, ...), kind=kOutput, calls=%fused_computation.19 | convolution fusion | flops 1612316672 | bytes 10380288 | tf_op jit(solution)/shard_map/tab,tk->kab/dot_general | solution.py:56
  275.4 22.4 %all-reduce.1 = f32[64,64]{0,1:T(8,128)S(1)} all-reduce(f32[64,64]{0,1:T(8,128)S(1)} %convolution_bitcast_fusion.2), channel_id=5, replica_groups=mesh['lat'=8,'lon'=4] {'lat'}, use_global_device_ids=true, to_apply=%region_8.11.clone | all-reduce | flops 4096 | bytes 32768
  297.9 15.8 %psum.45 = f32[8,64]{0,1:T(8,128)S(1)} all-reduce(f32[8,64]{0,1:T(8,128)S(1)} %constant_dynamic-slice_fusion.1), channel_id=1, replica_groups=mesh['lat'=8,'lon'=4] {'lon'}, use_global_device_ids=true, to_apply=%region_9.12 | all-reduce | flops 512 | bytes 4096 | tf_op jit(solution)/shard_map/psum | solution.py:72
  331.2 5.8 %cholesky.55 = f32[64,64]{1,0:T(8,128)S(1)} custom-call(f32[64,64]{1,0:T(8,128)S(1)} %fusion.74), custom_call_target="Cholesky" | custom-call | tf_op jit(solution)/shard_map/jit(cholesky)/cholesky | solution.py:88
  338.3 4.9 custom-call.7
  345.5 12.8 %fusion.45 = f32[1024,64]{0,1:T(8,128)} fusion(f32[1024,16,128]{2,1,0:T(8,128)} %param.7, f32[64,2048]{1,0:T(8,128)S(1)} %fusion.48), kind=kOutput, calls=%fused_computation.24 | convolution fusion | flops 1610612736 | bytes 9175040 | tf_op jit(solution)/shard_map/tab,kab->tk/dot_general | solution.py:52
  363.4 4.6 collective-permute-start.46
  369.6 23.1 %reduce-scatter.11.cloned.1.call-done = f32[128,64]{0,1:T(8,128)} async-done(((f32[1024,64]{0,1:T(8,128)}), f32[128,64]{0,1:T(8,128)}) %reduce-scatter.11.cloned.1.call-update) | async-done | bytes 32784 | tf_op jit(solution)/shard_map/reduce_scatter | solution.py:71
  392.7 19.6 %psum.46 = f32[128,64]{0,1:T(8,128)S(1)} all-reduce(f32[128,64]{0,1:T(8,128)} %reduce-scatter.11.cloned.1.call-done), channel_id=1, replica_groups=mesh['lat'=8,'lon'=4] {'lon'}, use_global_device_ids=true, to_apply=%region_11.14 | all-reduce | flops 8192 | bytes 65536 | tf_op jit(solution)/shard_map/psum | solution.py:72
  416.6 2.7 collective-permute-start.39
  425.3 4.2 collective-permute-done.42
  429.4 9.8 %fusion.30 = f32[64,16,128]{2,0,1:T(8,128)S(1)} fusion(f32[1024,16,128]{2,1,0:T(8,128)} %param.7, f32[64,18,128]{2,0,1:T(8,128)S(1)} %constant_dynamic-update-slice_fusion.3, f32[64,18,1]{2,0,1:T(8,128)S(1)} %copy.85, f32[64,18,1]{2,0,1:T(8,128)S(1)} %copy.83, f32[64,16,128]{2,0,1:T(8,128)S(1)} %copy_bitcast_fusion, ...), kind=kOutput, calls=%fused_computation.18 | convolution fusion | flops 1612316672 | bytes 10380288 | tf_op jit(solution)/shard_map/tab,tk->kab/dot_general | solution.py:56
  439.9 22.4 %all-reduce.2 = f32[64,64]{0,1:T(8,128)S(1)} all-reduce(f32[64,64]{0,1:T(8,128)S(1)} %convolution_bitcast_fusion.1), channel_id=7, replica_groups=mesh['lat'=8,'lon'=4] {'lat'}, use_global_device_ids=true, to_apply=%region_12.15.clone | all-reduce | flops 4096 | bytes 32768
  462.3 15.8 %psum.47 = f32[8,64]{0,1:T(8,128)S(1)} all-reduce(f32[8,64]{0,1:T(8,128)S(1)} %constant_dynamic-slice_fusion), channel_id=1, replica_groups=mesh['lat'=8,'lon'=4] {'lon'}, use_global_device_ids=true, to_apply=%region_13.16 | all-reduce | flops 512 | bytes 4096 | tf_op jit(solution)/shard_map/psum | solution.py:72
  (215 shorter events, 112.5 us)
Async XLA Ops:
  7.2 56.4 %reduce-scatter.7.cloned.1.call-start = ((), (), s32[]{:S(2)}) async-start(), calls=%async_computation.3 | async-start | bytes 294912 | tf_op jit(solution)/shard_map/reduce_scatter | solution.py:71
  9.2 17.3 %collective-permute-start.7 = (f32[64,1,128]{2,0,1:T(8,128)S(1)}, f32[64,1,128]{2,0,1:T(8,128)S(1)}, u32[]{:S(2)}, u32[]{:S(2)}) collective-permute-start(f32[64,1,128]{2,0,1:T(8,128)S(1)} %get-tuple-element.21), channel_id=1, source_target_pairs={{4,0},{8,4},{12,8},{16,12},{20,16},{24,20},{28,24},{5,1},{9,5},{13... | collective-permute-start | bytes 98312 | tf_op jit(solution)/shard_map/ppermute | solution.py:38
  10.5 16.0 %collective-permute-start.8 = (f32[64,1,128]{2,0,1:T(8,128)S(1)}, f32[64,1,128]{2,0,1:T(8,128)S(1)}, u32[]{:S(2)}, u32[]{:S(2)}) collective-permute-start(f32[64,1,128]{2,0,1:T(8,128)S(1)} %get-tuple-element.20), channel_id=1, source_target_pairs={{0,4},{4,8},{8,12},{12,16},{16,20},{20,24},{24,28},{1,5},{5,9},{9,... | collective-permute-start | bytes 98312 | tf_op jit(solution)/shard_map/ppermute | solution.py:35
  26.4 201.8 %reduce-scatter.9.cloned.1.call-start = ((), (), s32[]{:S(2)}) async-start(), calls=%async_computation.4 | async-start | bytes 294912 | tf_op jit(solution)/shard_map/reduce_scatter | solution.py:71
  27.0 8.5 %collective-permute-start.9 = (f32[64,18,1]{0,2,1:T(1,128)S(1)}, f32[64,18,1]{0,2,1:T(1,128)S(1)}, u32[]{:S(2)}, u32[]{:S(2)}) collective-permute-start(f32[64,18,1]{0,2,1:T(1,128)S(1)} %copy.51), channel_id=1, source_target_pairs={{1,0},{2,1},{3,2},{5,4},{6,5},{7,6},{9,8},{10,9},{11,10},{13,12},{... | collective-permute-start | bytes 13832 | tf_op jit(solution)/shard_map/ppermute | solution.py:38
  28.5 7.2 %collective-permute-start.10 = (f32[64,18,1]{0,2,1:T(1,128)S(1)}, f32[64,18,1]{0,2,1:T(1,128)S(1)}, u32[]{:S(2)}, u32[]{:S(2)}) collective-permute-start(f32[64,18,1]{0,2,1:T(1,128)S(1)} %copy.53), channel_id=1, source_target_pairs={{0,1},{1,2},{2,3},{4,5},{5,6},{6,7},{8,9},{9,10},{10,11},{12,13},{... | collective-permute-start | bytes 13832 | tf_op jit(solution)/shard_map/ppermute | solution.py:35
  83.2 4.3 collective-permute-start
  87.5 4.4 collective-permute-start.2
  87.5 4.4 collective-permute-start.3
  148.9 4.3 collective-permute-start.11
  157.5 7.4 %collective-permute-start.16 = (f32[8,64]{0,1:T(8,128)S(1)}, f32[8,64]{0,1:T(8,128)S(1)}, u32[]{:S(2)}, u32[]{:S(2)}) collective-permute-start(f32[8,64]{0,1:T(8,128)S(1)} %collective-permute-done.14), channel_id=1, source_target_pairs={{0,28},{4,0},{8,4},{12,8},{16,12},{20,16},{24,20},{28,24},{1,29},{... | collective-permute-start | bytes 6152 | tf_op jit(solution)/shard_map/ppermute | solution.py:23
  161.7 4.7 collective-permute-start.17
  179.7 15.5 %collective-permute-start.26 = (f32[64,1,128]{2,0,1:T(8,128)S(1)}, f32[64,1,128]{2,0,1:T(8,128)S(1)}, u32[]{:S(2)}, u32[]{:S(2)}) collective-permute-start(f32[64,1,128]{2,0,1:T(8,128)S(1)} %get-tuple-element.19), channel_id=1, source_target_pairs={{0,4},{4,8},{8,12},{12,16},{16,20},{20,24},{24,28},{1,5},{5,9},{9,... | collective-permute-start | bytes 98312 | tf_op jit(solution)/shard_map/ppermute | solution.py:35
  193.8 198.9 %reduce-scatter.11.cloned.1.call-start = ((), (), s32[]{:S(2)}) async-start(), calls=%async_computation.5 | async-start | bytes 294912 | tf_op jit(solution)/shard_map/reduce_scatter | solution.py:71
  197.4 6.1 %collective-permute-start.27 = (f32[64,18,1]{0,2,1:T(1,128)S(1)}, f32[64,18,1]{0,2,1:T(1,128)S(1)}, u32[]{:S(2)}, u32[]{:S(2)}) collective-permute-start(f32[64,18,1]{0,2,1:T(1,128)S(1)} %copy.66), channel_id=1, source_target_pairs={{1,0},{2,1},{3,2},{5,4},{6,5},{7,6},{9,8},{10,9},{11,10},{13,12},{... | collective-permute-start | bytes 13832 | tf_op jit(solution)/shard_map/ppermute | solution.py:38
  199.0 5.9 %collective-permute-start.28 = (f32[64,18,1]{0,2,1:T(1,128)S(1)}, f32[64,18,1]{0,2,1:T(1,128)S(1)}, u32[]{:S(2)}, u32[]{:S(2)}) collective-permute-start(f32[64,18,1]{0,2,1:T(1,128)S(1)} %copy.68), channel_id=1, source_target_pairs={{0,1},{1,2},{2,3},{4,5},{5,6},{6,7},{8,9},{9,10},{10,11},{12,13},{... | collective-permute-start | bytes 13832 | tf_op jit(solution)/shard_map/ppermute | solution.py:35
  247.8 4.3 collective-permute-start.18
  252.1 4.3 collective-permute-start.20
  252.1 4.3 collective-permute-start.21
  256.4 4.4 collective-permute-start.23
  260.7 4.4 collective-permute-start.24
  313.6 4.3 collective-permute-start.29
  322.2 6.8 %collective-permute-start.34 = (f32[8,64]{0,1:T(8,128)S(1)}, f32[8,64]{0,1:T(8,128)S(1)}, u32[]{:S(2)}, u32[]{:S(2)}) collective-permute-start(f32[8,64]{0,1:T(8,128)S(1)} %collective-permute-done.32), channel_id=1, source_target_pairs={{0,28},{4,0},{8,4},{12,8},{16,12},{20,16},{24,20},{28,24},{1,29},{... | collective-permute-start | bytes 6152 | tf_op jit(solution)/shard_map/ppermute | solution.py:23
  344.0 15.7 %collective-permute-start.44 = (f32[64,1,128]{2,0,1:T(8,128)S(1)}, f32[64,1,128]{2,0,1:T(8,128)S(1)}, u32[]{:S(2)}, u32[]{:S(2)}) collective-permute-start(f32[64,1,128]{2,0,1:T(8,128)S(1)} %get-tuple-element.17), channel_id=1, source_target_pairs={{0,4},{4,8},{8,12},{12,16},{16,20},{20,24},{24,28},{1,5},{5,9},{9,... | collective-permute-start | bytes 98312 | tf_op jit(solution)/shard_map/ppermute | solution.py:35
  361.9 6.1 %collective-permute-start.45 = (f32[64,18,1]{0,2,1:T(1,128)S(1)}, f32[64,18,1]{0,2,1:T(1,128)S(1)}, u32[]{:S(2)}, u32[]{:S(2)}) collective-permute-start(f32[64,18,1]{0,2,1:T(1,128)S(1)} %copy.82), channel_id=1, source_target_pairs={{1,0},{2,1},{3,2},{5,4},{6,5},{7,6},{9,8},{10,9},{11,10},{13,12},{... | collective-permute-start | bytes 13832 | tf_op jit(solution)/shard_map/ppermute | solution.py:38
  363.4 5.9 %collective-permute-start.46 = (f32[64,18,1]{0,2,1:T(1,128)S(1)}, f32[64,18,1]{0,2,1:T(1,128)S(1)}, u32[]{:S(2)}, u32[]{:S(2)}) collective-permute-start(f32[64,18,1]{0,2,1:T(1,128)S(1)} %copy.84), channel_id=1, source_target_pairs={{0,1},{1,2},{2,3},{4,5},{5,6},{6,7},{8,9},{9,10},{10,11},{12,13},{... | collective-permute-start | bytes 13832 | tf_op jit(solution)/shard_map/ppermute | solution.py:35
  412.3 4.3 collective-permute-start.36
  416.6 4.3 collective-permute-start.38
  416.6 4.3 collective-permute-start.39
  421.0 4.3 collective-permute-start.41
  478.1 4.3 collective-permute-start.47
  486.6 7.7 %collective-permute-start.52 = (f32[8,64]{0,1:T(8,128)S(1)}, f32[8,64]{0,1:T(8,128)S(1)}, u32[]{:S(2)}, u32[]{:S(2)}) collective-permute-start(f32[8,64]{0,1:T(8,128)S(1)} %collective-permute-done.50), channel_id=1, source_target_pairs={{0,28},{4,0},{8,4},{12,8},{16,12},{20,16},{24,20},{28,24},{1,29},{... | collective-permute-start | bytes 6152 | tf_op jit(solution)/shard_map/ppermute | solution.py:23
  (27 other events, 221.9 us)
Sparse Core Ops, SparseCore 0:
  26.5 37.0 reduce-scatter.6
  194.0 34.1 reduce-scatter.8
  358.4 34.2 reduce-scatter.10
